TPU v7x, 32 devices: a whole 2x2x4 slice. The times are simulated.
32 devices in a mesh: row: 8 (over y, x, core), col: 4 (over z).
Axes of the slice: x: 2, y: 2, z: 4, core: 2. Of those that a mesh axis runs over, the one named last changes fastest.
Arguments:
- vectors: bfloat16 [4, 16384], P(None, ('row', 'col')), may hold values from -6 to 6
- tile_values: bfloat16 [8, 4, 32, 4096], P('row', 'col'), may hold values from -0.75 to 0.75
- tile_rows: int32 [8, 4, 32], P('row', 'col'), may hold values from 0 to 31, as said below
- tile_cols: int32 [8, 4, 32], P('row', 'col'), may hold values from 0 to 63
- tile_scale: int32 [8, 4, 32], P('row', 'col'), may hold values from 0 to 63
- tile_count: int32 [8, 4], P('row', 'col'), may hold values from 2 to 32, as said below
- scale_table: float32 [64], replicated, may hold values from 0.1 to 1.5
Outputs:
- product: float32 [4, 16384], P(None, ('row', 'col'))
Inputs may be any that keep to these rules, and one draw needn't show every extreme that they name: Slots 0 to tile_count - 1 of a device hold its tiles, later slots are ignored; some device has all 32 slots live. On device (r, c), each slot t below min(8, 2) holds a diagonal block: tile_rows[r, c, t] = c * 8 + t; the other slots are uniform over the range.
All inputs are finite; a program needn't handle non-finite values.
Results may differ from a plain program's by a relative error of at most 0.0003.
Values may be sent and summed in bfloat16 or wider, within the bound.
A program may use at most 64 MiB of HBM per device.

v0:
```python
import functools

import jax
import jax.numpy as jnp
from jax import lax
from jax.experimental import pallas as pl
from jax.experimental.pallas import tpu as pltpu
from jax.sharding import PartitionSpec as P

TILE = 64
NVEC = 4
LANES = 128
GROUP = 4
MESH = pl.DeviceIdType.MESH


def relayout(slots, tv_vm, w32_vm, w_vm):
    pack = LANES // TILE
    step = max(1, 2 * LANES // (pack * slots))
    depth = pack * step * slots
    r = lax.broadcasted_iota(jnp.int32, (depth, depth), 0)
    c = lax.broadcasted_iota(jnp.int32, (depth, depth), 1)
    slot, i = lax.div(r, pack * step), lax.rem(r, pack * step)
    source = (lax.rem(i, pack) * step + lax.div(i, pack)) * slots + slot
    order = jnp.where(c == source, 1.0, 0.0).astype(jnp.bfloat16)
    low_half = lax.broadcasted_iota(jnp.int32, (slots, LANES), 1) < TILE
    total = TILE * TILE // LANES
    for first in range(0, total, step):
        low, high = [], []
        for g in range(first, first + step):
            part = tv_vm[:, g * LANES:(g + 1) * LANES].astype(jnp.float32)
            turned = pltpu.roll(part, TILE, 1)
            low.append(jnp.where(low_half, part, turned).astype(jnp.bfloat16))
            high.append(jnp.where(low_half, turned, part).astype(jnp.bfloat16))
        moved = jnp.dot(
            order, jnp.concatenate(low + high, axis=0), preferred_element_type=jnp.float32)
        w32_vm[:, first * pack:(first + step) * pack, :] = moved.reshape(
            slots, pack * step, LANES)
    w_vm[...] = w32_vm[...].reshape(slots * TILE, LANES).astype(jnp.bfloat16)


def kernel(
    n_row, n_col, slots, piece_len,
    x_hbm, w_hbm, rows_hbm, cols_hbm, scale_hbm, count_hbm, table_hbm,
    out_ref,
    col_x, row_x, tv_vm, w32_vm, w_vm, rows_sm, cols_sm, scale_sm, count_sm, table_sm,
    rid_vm, cid_vm, wt_vm, row_send, row_recv, col_send, col_recv,
    local_sem, x_row_send, x_row_recv, x_col_send, x_col_recv,
    p_row_send, p_row_recv, p_col_send, p_col_recv,
):
    me_row = lax.axis_index("row")
    me_col = lax.axis_index("col")
    blocks = piece_len // TILE
    chunk = piece_len * NVEC // LANES
    depth = slots * NVEC

    copies = [
        pltpu.make_async_copy(src, dst, local_sem.at[i])
        for i, (src, dst) in enumerate((
            (x_hbm, col_x.at[0]),
            (x_hbm, row_x.at[0]),
            (rows_hbm, rows_sm),
            (cols_hbm, cols_sm),
            (scale_hbm, scale_sm),
            (count_hbm, count_sm),
            (table_hbm, table_sm),
            (w_hbm, tv_vm),
        ))
    ]
    for copy in copies:
        copy.start()

    def along_col(d):
        return (me_row, lax.rem(me_col + d, n_col))

    def along_row(d):
        return (lax.rem(me_row + d, n_row), me_col)

    barrier = pltpu.get_barrier_semaphore()
    for d in range(1, n_col):
        pl.semaphore_signal(barrier, inc=1, device_id=along_col(d), device_id_type=MESH)
    for d in range(1, n_row):
        pl.semaphore_signal(barrier, inc=1, device_id=along_row(d), device_id_type=MESH)
    copies[0].wait()
    copies[1].wait()
    pl.semaphore_wait(barrier, n_col + n_row - 2)

    gather_row = [
        pltpu.make_async_remote_copy(
            src_ref=row_x.at[0], dst_ref=row_x.at[d], send_sem=x_row_send.at[d],
            recv_sem=x_row_recv.at[d], device_id=along_col(d), device_id_type=MESH)
        for d in range(1, n_col)
    ]
    gather_col = [
        pltpu.make_async_remote_copy(
            src_ref=col_x.at[0], dst_ref=col_x.at[d], send_sem=x_col_send.at[d],
            recv_sem=x_col_recv.at[d], device_id=along_row(d), device_id_type=MESH)
        for d in range(1, n_row)
    ]
    for copy in gather_row + gather_col:
        copy.start()

    copies[7].wait()
    relayout(slots, tv_vm, w32_vm, w_vm)
    for copy in copies[2:7]:
        copy.wait()
    upper = lax.broadcasted_iota(jnp.int32, (8, LANES), 0) < NVEC
    for v in range(slots // 2):
        a, b = 2 * v, 2 * v + 1
        here = pl.ds(8 * v, 8)
        rid_vm[here, :] = jnp.where(upper, rows_sm[0, 0, a], rows_sm[0, 0, b])
        cid_vm[here, :] = jnp.where(upper, cols_sm[0, 0, a], cols_sm[0, 0, b])
        wt_vm[here, :] = jnp.where(
            upper, table_sm[scale_sm[0, 0, a]], table_sm[scale_sm[0, 0, b]])
    rid = rid_vm[...]
    cid = cid_vm[...]
    sub = lax.broadcasted_iota(jnp.int32, (depth, LANES), 0)
    lane = lax.broadcasted_iota(jnp.int32, (depth, LANES), 1)
    half = lax.div(lane, TILE)
    rid_piece, rid_block = lax.div(rid, blocks), lax.rem(rid, blocks)
    cid_piece, cid_block = lax.div(cid, blocks), lax.rem(cid, blocks)
    global_row = me_row * (n_col * blocks) + rid
    global_col = (cid_piece * n_col + me_col) * blocks + cid_block
    weight = jnp.where(global_row == global_col, 0.5, 1.0) * wt_vm[...]
    weight = jnp.where(lax.div(sub, NVEC) < count_sm[0, 0], weight, 0.0)

    def places(piece, block, me, total):
        back = lax.rem(me - piece + total, total)
        target = back * chunk + lax.div(block, 2) * NVEC + lax.rem(sub, NVEC)
        across = lax.broadcasted_iota(jnp.int32, (depth, total * chunk), 1)
        down = lax.broadcasted_iota(jnp.int32, (total * chunk, depth), 0)
        take = jnp.where(across == target[:, :1], 1.0, 0.0).astype(jnp.bfloat16)
        put = jnp.where(down == jnp.transpose(target)[:1, :], 1.0, 0.0).astype(jnp.bfloat16)
        return take, jnp.concatenate([put, put], axis=1), lax.rem(block, 2)

    take_row, put_row, odd_row = places(rid_piece, rid_block, me_col, n_col)
    take_col, put_col, odd_col = places(cid_piece, cid_block, me_row, n_row)
    row_weight = jnp.where(half == odd_row, weight, 0.0)
    col_weight = jnp.where(half == odd_col, weight, 0.0)

    def pick(take, pieces, odd):
        both = jnp.dot(take, pieces, preferred_element_type=jnp.float32)
        kept = jnp.where(half == odd, both, 0.0)
        return (kept + pltpu.roll(kept, TILE, 1)).astype(jnp.bfloat16)

    def place(put, values):
        high = values.astype(jnp.bfloat16)
        low = (values - high.astype(jnp.float32)).astype(jnp.bfloat16)
        return jnp.dot(
            put, jnp.concatenate([high, low], axis=0), preferred_element_type=jnp.float32)

    rows_of = GROUP * NVEC
    wide = GROUP * TILE
    g_row = lax.div(lax.broadcasted_iota(jnp.int32, (rows_of, wide), 0), NVEC)
    g_col = lax.div(lax.broadcasted_iota(jnp.int32, (rows_of, wide), 1), TILE)
    same = g_row == g_col

    for copy in gather_col:
        copy.wait_recv()
    distant = pick(take_col, col_x[...].reshape(n_row * chunk, LANES), odd_col)
    parts = []
    for g in range(slots // GROUP):
        tiles = w_vm[g * wide:(g + 1) * wide, :]
        prod = lax.dot_general(
            distant[g * rows_of:(g + 1) * rows_of, :TILE], tiles[:, :TILE],
            (((1,), (1,)), ((), ())),
            preferred_element_type=jnp.float32)
        prod = jnp.where(same, prod, 0.0)
        total = prod[:, :LANES]
        for i in range(LANES, wide, LANES):
            total = total + prod[:, i:i + LANES]
        parts.append(total + pltpu.roll(total, TILE, 1))
    forward = jnp.concatenate(parts, axis=0) * row_weight
    row_send[...] = place(put_row, forward).reshape(n_col, chunk, LANES)
    scatter_row = [
        pltpu.make_async_remote_copy(
            src_ref=row_send.at[d], dst_ref=row_recv.at[d], send_sem=p_row_send.at[d],
            recv_sem=p_row_recv.at[d], device_id=along_col(n_col - d), device_id_type=MESH)
        for d in range(1, n_col)
    ]
    for copy in scatter_row:
        copy.start()

    for copy in gather_row:
        copy.wait_recv()
    near = pick(take_row, row_x[...].reshape(n_col * chunk, LANES), odd_row)
    parts = []
    for g in range(slots // GROUP):
        tiles = w_vm[g * wide:(g + 1) * wide, :]
        left = near[g * rows_of:(g + 1) * rows_of, :]
        left = jnp.concatenate([left] * (wide // LANES), axis=1)
        left = jnp.where(same, left, jnp.zeros_like(left))
        parts.append(jnp.dot(left, tiles, preferred_element_type=jnp.float32))
    mirrored = jnp.concatenate(parts, axis=0) * col_weight
    col_send[...] = place(put_col, mirrored).reshape(n_row, chunk, LANES)
    scatter_col = [
        pltpu.make_async_remote_copy(
            src_ref=col_send.at[d], dst_ref=col_recv.at[d], send_sem=p_col_send.at[d],
            recv_sem=p_col_recv.at[d], device_id=along_row(n_row - d), device_id_type=MESH)
        for d in range(1, n_row)
    ]
    for copy in scatter_col:
        copy.start()

    total = row_send[0] + col_send[0]
    for copy in gather_row + gather_col:
        copy.wait_send()
    for d, copy in enumerate(scatter_row, 1):
        copy.wait_recv()
        total = total + row_recv[d]
    for d, copy in enumerate(scatter_col, 1):
        copy.wait_recv()
        total = total + col_recv[d]
    out_ref[...] = total
    for copy in scatter_row + scatter_col:
        copy.wait_send()


def per_device(vectors, tile_values, tile_rows, tile_cols, tile_scale, tile_count, scale_table):
    n_row = lax.axis_size("row")
    n_col = lax.axis_size("col")
    piece_len = vectors.shape[1]
    slots = tile_rows.shape[-1]
    groups = piece_len // LANES
    chunk = groups * NVEC
    depth = slots * NVEC
    x = vectors.reshape(NVEC, groups, LANES).transpose(1, 0, 2).reshape(chunk, LANES)
    w = tile_values.reshape(slots, TILE * TILE)
    dma = pltpu.SemaphoreType.DMA
    out = pl.pallas_call(
        functools.partial(kernel, n_row, n_col, slots, piece_len),
        out_shape=pltpu.VMEM((chunk, LANES), jnp.float32),
        in_specs=[pl.BlockSpec(memory_space=pltpu.HBM)] * 7,
        out_specs=pl.BlockSpec(memory_space=pltpu.VMEM),
        scratch_shapes=[
            pltpu.VMEM((n_row, chunk, LANES), jnp.bfloat16),
            pltpu.VMEM((n_col, chunk, LANES), jnp.bfloat16),
            pltpu.VMEM((slots, TILE * TILE), jnp.bfloat16),
            pltpu.VMEM((slots, TILE, LANES), jnp.float32),
            pltpu.VMEM((slots * TILE, LANES), jnp.bfloat16),
            pltpu.SMEM(tile_rows.shape, jnp.int32),
            pltpu.SMEM(tile_cols.shape, jnp.int32),
            pltpu.SMEM(tile_scale.shape, jnp.int32),
            pltpu.SMEM(tile_count.shape, jnp.int32),
            pltpu.SMEM(scale_table.shape, jnp.float32),
            pltpu.VMEM((depth, LANES), jnp.int32),
            pltpu.VMEM((depth, LANES), jnp.int32),
            pltpu.VMEM((depth, LANES), jnp.float32),
            pltpu.VMEM((n_col, chunk, LANES), jnp.float32),
            pltpu.VMEM((n_col, chunk, LANES), jnp.float32),
            pltpu.VMEM((n_row, chunk, LANES), jnp.float32),
            pltpu.VMEM((n_row, chunk, LANES), jnp.float32),
            dma((8,)),
            dma((n_col,)), dma((n_col,)), dma((n_row,)), dma((n_row,)),
            dma((n_col,)), dma((n_col,)), dma((n_row,)), dma((n_row,)),
        ],
        compiler_params=pltpu.CompilerParams(collective_id=0, has_side_effects=True),
        name="lanczos",
    )(x, w, tile_rows, tile_cols, tile_scale, tile_count, scale_table)
    return out.reshape(groups, NVEC, LANES).transpose(1, 0, 2).reshape(NVEC, piece_len)


def solution(mesh):
    return jax.shard_map(
        per_device,
        mesh=mesh,
        in_specs=(
            P(None, ("row", "col")),
            P("row", "col", None, None),
            P("row", "col", None),
            P("row", "col", None),
            P("row", "col", None),
            P("row", "col"),
            P(),
        ),
        out_specs=P(None, ("row", "col")),
        check_vma=False,
    )
```

profile of v0, /device:TPU:0, one launch (start us, length us, event | category | flops | bytes accessed | tf_op | source)
XLA Modules:
  0.0 14.6 jit_solution(12543822970396079820)
XLA Ops:
  0.7 13.4 %lanczos.1 = f32[16,128]{1,0:T(8,128)S(1)} custom-call(bf16[16,128]{1,0:T(8,128)(2,1)} %bitcast.13, bf16[32,4096]{1,0:T(8,128)(2,1)} %bitcast.12, s32[1,1,32]{2,1,0:T(1,128)} %rows_hbm.1, s32[1,1,32]{2,1,0:T(1,128)} %cols_hbm.1, s32[1,1,32]{2,1,0:T(1,128)} %scale_hbm.1, s32[1,1]{1,0:T(1,128)S(6)} %copy.12.count_hbm, f32[64]{0:T(128)} %table_hbm.1), custom_call_target="tpu_custom_call" | custom-call | tf_op jit(solution)/shard_map/lanczos/pallas_call | solution.py:230
  14.0 0.6 %copy.11 = f32[4,512]{1,0:T(4,128)} copy(f32[4,512]{1,0:T(4,128)S(1)} %bitcast.11) | data formatting | bytes 16384
where the time goes:
time: 14.8 us; the launch traced here: 14.6 us
  Pallas kernels  13.4 us (91%)
  between operations  0.66 us (4%)
  local copies, waits for them, and re-layouts  0.6 us (4%)
    pallas_call x1, Pallas kernels, per_device(): pl.pallas_call(functools.partial(kernel, n_row, n_col, slots, piece_len),...  13.4 us
    unnamed x1, local copies, waits for them, and re-layouts  0.6 us

commit v1 on v0

v1 whole, which is shorter than its diff:
```python
import functools

import jax
import jax.numpy as jnp
from jax import lax
from jax.experimental import pallas as pl
from jax.experimental.pallas import tpu as pltpu
from jax.sharding import PartitionSpec as P

TILE = 64
NVEC = 4
LANES = 128
GROUP = 4
MESH = pl.DeviceIdType.MESH


def relayout(slots, tv_vm, w32_vm, w_vm):
    pack = LANES // TILE
    step = max(1, 2 * LANES // (pack * slots))
    depth = pack * step * slots
    r = lax.broadcasted_iota(jnp.int32, (depth, depth), 0)
    c = lax.broadcasted_iota(jnp.int32, (depth, depth), 1)
    slot, i = lax.div(r, pack * step), lax.rem(r, pack * step)
    source = (lax.rem(i, pack) * step + lax.div(i, pack)) * slots + slot
    order = jnp.where(c == source, 1.0, 0.0).astype(jnp.bfloat16)
    low_half = lax.broadcasted_iota(jnp.int32, (slots, LANES), 1) < TILE
    total = TILE * TILE // LANES
    for first in range(0, total, step):
        low, high = [], []
        for g in range(first, first + step):
            part = tv_vm[:, g * LANES:(g + 1) * LANES].astype(jnp.float32)
            turned = pltpu.roll(part, TILE, 1)
            low.append(jnp.where(low_half, part, turned).astype(jnp.bfloat16))
            high.append(jnp.where(low_half, turned, part).astype(jnp.bfloat16))
        moved = jnp.dot(
            order, jnp.concatenate(low + high, axis=0), preferred_element_type=jnp.float32)
        w32_vm[:, first * pack:(first + step) * pack, :] = moved.reshape(
            slots, pack * step, LANES)
    w_vm[...] = w32_vm[...].reshape(slots * TILE, LANES).astype(jnp.bfloat16)


def kernel(
    n_row, n_col, slots, piece_len,
    x_hbm, w_hbm, rows_hbm, cols_hbm, scale_hbm, count_sm, table_hbm,
    out_ref,
    x_vm, tv_vm, w32_vm, w_vm, rows_sm, cols_sm, scale_sm, table_sm,
    rid_vm, cid_vm, wt_vm, row_send, col_send, part_vm,
    ready_sem, local_sem, x_send, x_row_sem, x_col_sem, p_send, p_row_sem, p_col_sem,
):
    me_row = lax.axis_index("row")
    me_col = lax.axis_index("col")
    blocks = piece_len // TILE
    chunk = piece_len * NVEC // LANES
    depth = slots * NVEC
    peers = n_row + n_col - 2
    row_x = x_vm.at[pl.ds(0, n_col)]
    col_x = x_vm.at[pl.ds(n_col, n_row)]

    def along_col(p):
        return (me_row, p)

    def along_row(p):
        return (p, me_col)

    def each(low, act):
        for me, total, place in ((me_col, n_col, along_col), (me_row, n_row, along_row)):
            for p in range(total):
                if (low and p < total - 1) or (not low and p > 0):
                    pl.when(p < me if low else p > me)(
                        functools.partial(act, p, place, place is along_col))

    barrier = pltpu.get_barrier_semaphore()

    def enter(p, place, is_col):
        pl.semaphore_signal(barrier, inc=1, device_id=place(p), device_id_type=MESH)

    def answer(p, place, is_col):
        pl.semaphore_signal(ready_sem, inc=1, device_id=place(p), device_id_type=MESH)

    def spread(p, place, is_col):
        slot = me_col if is_col else n_col + me_row
        pltpu.make_async_remote_copy(
            src_ref=x_hbm, dst_ref=x_vm.at[slot], send_sem=x_send,
            recv_sem=x_row_sem if is_col else x_col_sem,
            device_id=place(p), device_id_type=MESH).start()

    each(False, enter)
    lower = me_row + me_col

    @pl.when(lower > 0)
    def _():
        pl.semaphore_wait(barrier, lower)

    each(True, spread)
    each(True, answer)
    copies = [
        pltpu.make_async_copy(src, dst, local_sem.at[i])
        for i, (src, dst) in enumerate((
            (w_hbm, tv_vm),
            (rows_hbm, rows_sm),
            (cols_hbm, cols_sm),
            (scale_hbm, scale_sm),
            (table_hbm, table_sm),
        ))
    ]
    pltpu.make_async_copy(x_hbm, x_vm.at[me_col], x_row_sem).start()
    pltpu.make_async_copy(x_hbm, x_vm.at[n_col + me_row], x_col_sem).start()
    for copy in copies:
        copy.start()

    @pl.when(lower < peers)
    def _():
        pl.semaphore_wait(ready_sem, peers - lower)

    each(False, spread)

    copies[0].wait()
    relayout(slots, tv_vm, w32_vm, w_vm)
    for copy in copies[1:]:
        copy.wait()
    upper = lax.broadcasted_iota(jnp.int32, (8, LANES), 0) < NVEC
    for v in range(slots // 2):
        a, b = 2 * v, 2 * v + 1
        here = pl.ds(8 * v, 8)
        rid_vm[here, :] = jnp.where(upper, rows_sm[0, 0, a], rows_sm[0, 0, b])
        cid_vm[here, :] = jnp.where(upper, cols_sm[0, 0, a], cols_sm[0, 0, b])
        wt_vm[here, :] = jnp.where(
            upper, table_sm[scale_sm[0, 0, a]], table_sm[scale_sm[0, 0, b]])
    rid = rid_vm[...]
    cid = cid_vm[...]
    sub = lax.broadcasted_iota(jnp.int32, (depth, LANES), 0)
    lane = lax.broadcasted_iota(jnp.int32, (depth, LANES), 1)
    half = lax.div(lane, TILE)
    rid_piece, rid_block = lax.div(rid, blocks), lax.rem(rid, blocks)
    cid_piece, cid_block = lax.div(cid, blocks), lax.rem(cid, blocks)
    global_row = me_row * (n_col * blocks) + rid
    global_col = (cid_piece * n_col + me_col) * blocks + cid_block
    weight = jnp.where(global_row == global_col, 0.5, 1.0) * wt_vm[...]
    weight = jnp.where(lax.div(sub, NVEC) < count_sm[0, 0], weight, 0.0)

    def places(piece, block, total):
        target = piece * chunk + lax.div(block, 2) * NVEC + lax.rem(sub, NVEC)
        across = lax.broadcasted_iota(jnp.int32, (depth, total * chunk), 1)
        down = lax.broadcasted_iota(jnp.int32, (total * chunk, depth), 0)
        take = jnp.where(across == target[:, :1], 1.0, 0.0).astype(jnp.bfloat16)
        put = jnp.where(down == jnp.transpose(target)[:1, :], 1.0, 0.0).astype(jnp.bfloat16)
        return take, jnp.concatenate([put, put], axis=1), lax.rem(block, 2)

    take_row, put_row, odd_row = places(rid_piece, rid_block, n_col)
    take_col, put_col, odd_col = places(cid_piece, cid_block, n_row)
    row_weight = jnp.where(half == odd_row, weight, 0.0)
    col_weight = jnp.where(half == odd_col, weight, 0.0)

    def pick(take, pieces, odd):
        both = jnp.dot(take, pieces, preferred_element_type=jnp.float32)
        kept = jnp.where(half == odd, both, 0.0)
        return (kept + pltpu.roll(kept, TILE, 1)).astype(jnp.bfloat16)

    def place(put, values):
        high = values.astype(jnp.bfloat16)
        low = (values - high.astype(jnp.float32)).astype(jnp.bfloat16)
        return jnp.dot(
            put, jnp.concatenate([high, low], axis=0), preferred_element_type=jnp.float32)

    rows_of = GROUP * NVEC
    wide = GROUP * TILE
    g_row = lax.div(lax.broadcasted_iota(jnp.int32, (rows_of, wide), 0), NVEC)
    g_col = lax.div(lax.broadcasted_iota(jnp.int32, (rows_of, wide), 1), TILE)
    same = g_row == g_col

    def scatter(me, total, where, source, first, sem):
        for k in range(total - 1):
            p = k + jnp.where(me <= k, 1, 0)
            slot = first + lax.rem(me - p + total, total) - 1
            pltpu.make_async_remote_copy(
                src_ref=source.at[p], dst_ref=part_vm.at[slot], send_sem=p_send,
                recv_sem=sem, device_id=where(p), device_id_type=MESH).start()

    def forward():
        pltpu.make_async_copy(col_x, col_x, x_col_sem).wait()
        distant = pick(take_col, col_x[...].reshape(n_row * chunk, LANES), odd_col)
        parts = []
        for g in range(slots // GROUP):
            tiles = w_vm[g * wide:(g + 1) * wide, :]
            prod = lax.dot_general(
                distant[g * rows_of:(g + 1) * rows_of, :TILE], tiles[:, :TILE],
                (((1,), (1,)), ((), ())),
                preferred_element_type=jnp.float32)
            prod = jnp.where(same, prod, 0.0)
            total = prod[:, :LANES]
            for i in range(LANES, wide, LANES):
                total = total + prod[:, i:i + LANES]
            parts.append(total + pltpu.roll(total, TILE, 1))
        values = jnp.concatenate(parts, axis=0) * row_weight
        row_send[...] = place(put_row, values).reshape(n_col, chunk, LANES)
        scatter(me_col, n_col, along_col, row_send, 0, p_row_sem)

    def mirrored():
        pltpu.make_async_copy(row_x, row_x, x_row_sem).wait()
        near = pick(take_row, row_x[...].reshape(n_col * chunk, LANES), odd_row)
        parts = []
        for g in range(slots // GROUP):
            tiles = w_vm[g * wide:(g + 1) * wide, :]
            left = near[g * rows_of:(g + 1) * rows_of, :]
            left = jnp.concatenate([left] * (wide // LANES), axis=1)
            left = jnp.where(same, left, jnp.zeros_like(left))
            parts.append(jnp.dot(left, tiles, preferred_element_type=jnp.float32))
        values = jnp.concatenate(parts, axis=0) * col_weight
        col_send[...] = place(put_col, values).reshape(n_row, chunk, LANES)
        scatter(me_row, n_row, along_row, col_send, n_col - 1, p_col_sem)

    @pl.when(me_col == 0)
    def _():
        mirrored()
        forward()

    @pl.when(me_col > 0)
    def _():
        forward()
        mirrored()

    total = row_send[me_col] + col_send[me_row]
    got_row = part_vm.at[pl.ds(0, n_col - 1)]
    got_col = part_vm.at[pl.ds(n_col - 1, n_row - 1)]
    sent_x = x_vm.at[pl.ds(0, peers)]
    pltpu.make_async_copy(sent_x, sent_x, x_send).wait()
    pltpu.make_async_copy(got_row, got_row, p_row_sem).wait()
    for d in range(n_col - 1):
        total = total + part_vm[d]
    pltpu.make_async_copy(got_col, got_col, p_col_sem).wait()
    for d in range(n_col - 1, peers):
        total = total + part_vm[d]
    out_ref[...] = total
    pltpu.make_async_copy(part_vm, part_vm, p_send).wait()


def per_device(vectors, tile_values, tile_rows, tile_cols, tile_scale, tile_count, scale_table):
    n_row = lax.axis_size("row")
    n_col = lax.axis_size("col")
    piece_len = vectors.shape[1]
    slots = tile_rows.shape[-1]
    groups = piece_len // LANES
    chunk = groups * NVEC
    depth = slots * NVEC
    x = vectors.reshape(NVEC, groups, LANES).transpose(1, 0, 2).reshape(chunk, LANES)
    w = tile_values.reshape(slots, TILE * TILE)
    dma = pltpu.SemaphoreType.DMA
    hbm = pl.BlockSpec(memory_space=pltpu.HBM)
    out = pl.pallas_call(
        functools.partial(kernel, n_row, n_col, slots, piece_len),
        out_shape=pltpu.VMEM((chunk, LANES), jnp.float32),
        in_specs=[hbm] * 5 + [pl.BlockSpec(memory_space=pltpu.SMEM), hbm],
        out_specs=pl.BlockSpec(memory_space=pltpu.VMEM),
        scratch_shapes=[
            pltpu.VMEM((n_col + n_row, chunk, LANES), jnp.bfloat16),
            pltpu.VMEM((slots, TILE * TILE), jnp.bfloat16),
            pltpu.VMEM((slots, TILE, LANES), jnp.float32),
            pltpu.VMEM((slots * TILE, LANES), jnp.bfloat16),
            pltpu.SMEM(tile_rows.shape, jnp.int32),
            pltpu.SMEM(tile_cols.shape, jnp.int32),
            pltpu.SMEM(tile_scale.shape, jnp.int32),
            pltpu.SMEM(scale_table.shape, jnp.float32),
            pltpu.VMEM((depth, LANES), jnp.int32),
            pltpu.VMEM((depth, LANES), jnp.int32),
            pltpu.VMEM((depth, LANES), jnp.float32),
            pltpu.VMEM((n_col, chunk, LANES), jnp.float32),
            pltpu.VMEM((n_row, chunk, LANES), jnp.float32),
            pltpu.VMEM((n_col + n_row - 2, chunk, LANES), jnp.float32),
            pltpu.SemaphoreType.REGULAR,
            dma((5,)), dma, dma, dma, dma, dma, dma,
        ],
        compiler_params=pltpu.CompilerParams(collective_id=0, has_side_effects=True),
        name="lanczos",
    )(x, w, tile_rows, tile_cols, tile_scale, tile_count, scale_table)
    return out.reshape(groups, NVEC, LANES).transpose(1, 0, 2).reshape(NVEC, piece_len)


def solution(mesh):
    return jax.shard_map(
        per_device,
        mesh=mesh,
        in_specs=(
            P(None, ("row", "col")),
            P("row", "col", None, None),
            P("row", "col", None),
            P("row", "col", None),
            P("row", "col", None),
            P("row", "col"),
            P(),
        ),
        out_specs=P(None, ("row", "col")),
        check_vma=False,
    )
```

time: 14.8 us -> 13.8 us (0.932)
  Pallas kernels: 13.4 us -> 12.4 us
    pallas_call x1, Pallas kernels: 13.4 us -> 12.4 us  [per_device(): pl.pallas_call(functools.partial(kernel, n_row, n_col, slots, piece_len),...]
where the time goes in v1:
time: 13.8 us; the launch traced here: 13.7 us
  Pallas kernels  12.4 us (90%)
  between operations  0.66 us (5%)
  local copies, waits for them, and re-layouts  0.6 us (4%)
    pallas_call x1, Pallas kernels, per_device(): pl.pallas_call(functools.partial(kernel, n_row, n_col, slots, piece_len),...  12.4 us
    unnamed x1, local copies, waits for them, and re-layouts  0.6 us

profile of v1, /device:TPU:0, one launch (start us, length us, event | category | flops | bytes accessed | tf_op | source)
XLA Modules:
  0.0 13.7 jit_solution(16310760235133881626)
XLA Ops:
  0.7 12.4 %lanczos.1 = f32[16,128]{1,0:T(8,128)S(1)} custom-call(bf16[16,128]{1,0:T(8,128)(2,1)} %bitcast.13, bf16[32,4096]{1,0:T(8,128)(2,1)} %bitcast.12, s32[1,1,32]{2,1,0:T(1,128)} %rows_hbm.1, s32[1,1,32]{2,1,0:T(1,128)} %cols_hbm.1, s32[1,1,32]{2,1,0:T(1,128)} %scale_hbm.1, s32[1,1]{1,0:T(1,128)S(6)} %copy.12.count_sm, f32[64]{0:T(128)} %table_hbm.1), custom_call_target="tpu_custom_call" | custom-call | tf_op jit(solution)/shard_map/lanczos/pallas_call | solution.py:249
  13.1 0.6 %copy.11 = f32[4,512]{1,0:T(4,128)} copy(f32[4,512]{1,0:T(4,128)S(1)} %bitcast.11) | data formatting | bytes 16384

commit v2 on v1

--- a/solution.py
+++ b/solution.py
@@ -43,9 +43,10 @@
     n_row, n_col, slots, piece_len,
     x_hbm, w_hbm, rows_hbm, cols_hbm, scale_hbm, count_sm, table_hbm,
     out_ref,
-    x_vm, tv_vm, w32_vm, w_vm, rows_sm, cols_sm, scale_sm, table_sm,
+    x_vm, tv_vm, w32_vm, w_vm, index_sm, table_sm,
     rid_vm, cid_vm, wt_vm, row_send, col_send, part_vm,
-    ready_sem, local_sem, x_send, x_row_sem, x_col_sem, p_send, p_row_sem, p_col_sem,
+    ready_sem, own_sem, tile_sem, index_sem, table_sem,
+    x_send, x_row_sem, x_col_sem, p_send, p_row_sem, p_col_sem,
 ):
     me_row = lax.axis_index("row")
     me_col = lax.axis_index("col")
@@ -80,11 +81,22 @@
     def spread(p, place, is_col):
         slot = me_col if is_col else n_col + me_row
         pltpu.make_async_remote_copy(
-            src_ref=x_hbm, dst_ref=x_vm.at[slot], send_sem=x_send,
+            src_ref=x_vm.at[me_col], dst_ref=x_vm.at[slot], send_sem=x_send,
             recv_sem=x_row_sem if is_col else x_col_sem,
             device_id=place(p), device_id_type=MESH).start()
 
+    own = pltpu.make_async_copy(x_hbm, x_vm.at[me_col], own_sem)
+    again = pltpu.make_async_copy(x_hbm, x_vm.at[n_col + me_row], x_col_sem)
+    tiles_in = pltpu.make_async_copy(w_hbm, tv_vm, tile_sem)
+    table_in = pltpu.make_async_copy(table_hbm, table_sm, table_sem)
+    own.start()
     each(False, enter)
+    again.start()
+    tiles_in.start()
+    for i, src in enumerate((rows_hbm, cols_hbm, scale_hbm)):
+        pltpu.make_async_copy(src, index_sm.at[i], index_sem).start()
+    table_in.start()
+    own.wait()
     lower = me_row + me_col
 
     @pl.when(lower > 0)
@@ -93,20 +105,6 @@
 
     each(True, spread)
     each(True, answer)
-    copies = [
-        pltpu.make_async_copy(src, dst, local_sem.at[i])
-        for i, (src, dst) in enumerate((
-            (w_hbm, tv_vm),
-            (rows_hbm, rows_sm),
-            (cols_hbm, cols_sm),
-            (scale_hbm, scale_sm),
-            (table_hbm, table_sm),
-        ))
-    ]
-    pltpu.make_async_copy(x_hbm, x_vm.at[me_col], x_row_sem).start()
-    pltpu.make_async_copy(x_hbm, x_vm.at[n_col + me_row], x_col_sem).start()
-    for copy in copies:
-        copy.start()
 
     @pl.when(lower < peers)
     def _():
@@ -114,18 +112,18 @@
 
     each(False, spread)
 
-    copies[0].wait()
+    tiles_in.wait()
     relayout(slots, tv_vm, w32_vm, w_vm)
-    for copy in copies[1:]:
-        copy.wait()
+    pltpu.make_async_copy(index_sm, index_sm, index_sem).wait()
+    table_in.wait()
     upper = lax.broadcasted_iota(jnp.int32, (8, LANES), 0) < NVEC
     for v in range(slots // 2):
         a, b = 2 * v, 2 * v + 1
         here = pl.ds(8 * v, 8)
-        rid_vm[here, :] = jnp.where(upper, rows_sm[0, 0, a], rows_sm[0, 0, b])
-        cid_vm[here, :] = jnp.where(upper, cols_sm[0, 0, a], cols_sm[0, 0, b])
+        rid_vm[here, :] = jnp.where(upper, index_sm[0, 0, 0, a], index_sm[0, 0, 0, b])
+        cid_vm[here, :] = jnp.where(upper, index_sm[1, 0, 0, a], index_sm[1, 0, 0, b])
         wt_vm[here, :] = jnp.where(
-            upper, table_sm[scale_sm[0, 0, a]], table_sm[scale_sm[0, 0, b]])
+            upper, table_sm[index_sm[2, 0, 0, a]], table_sm[index_sm[2, 0, 0, b]])
     rid = rid_vm[...]
     cid = cid_vm[...]
     sub = lax.broadcasted_iota(jnp.int32, (depth, LANES), 0)
@@ -196,7 +194,8 @@
         scatter(me_col, n_col, along_col, row_send, 0, p_row_sem)
 
     def mirrored():
-        pltpu.make_async_copy(row_x, row_x, x_row_sem).wait()
+        others = row_x.at[pl.ds(0, n_col - 1)]
+        pltpu.make_async_copy(others, others, x_row_sem).wait()
         near = pick(take_row, row_x[...].reshape(n_col * chunk, LANES), odd_row)
         parts = []
         for g in range(slots // GROUP):
@@ -256,9 +255,7 @@
             pltpu.VMEM((slots, TILE * TILE), jnp.bfloat16),
             pltpu.VMEM((slots, TILE, LANES), jnp.float32),
             pltpu.VMEM((slots * TILE, LANES), jnp.bfloat16),
-            pltpu.SMEM(tile_rows.shape, jnp.int32),
-            pltpu.SMEM(tile_cols.shape, jnp.int32),
-            pltpu.SMEM(tile_scale.shape, jnp.int32),
+            pltpu.SMEM((3,) + tile_rows.shape, jnp.int32),
             pltpu.SMEM(scale_table.shape, jnp.float32),
             pltpu.VMEM((depth, LANES), jnp.int32),
             pltpu.VMEM((depth, LANES), jnp.int32),
@@ -267,7 +264,7 @@
             pltpu.VMEM((n_row, chunk, LANES), jnp.float32),
             pltpu.VMEM((n_col + n_row - 2, chunk, LANES), jnp.float32),
             pltpu.SemaphoreType.REGULAR,
-            dma((5,)), dma, dma, dma, dma, dma, dma,
+            dma, dma, dma, dma, dma, dma, dma, dma, dma, dma,
         ],
         compiler_params=pltpu.CompilerParams(collective_id=0, has_side_effects=True),
         name="lanczos",

time: 13.8 us -> 13.6 us (0.986)
  Pallas kernels: 12.4 us -> 12.2 us
    pallas_call x1, Pallas kernels: 12.4 us -> 12.2 us  [per_device(): pl.pallas_call(functools.partial(kernel, n_row, n_col, slots, piece_len),...]
where the time goes in v2:
time: 13.6 us; the launch traced here: 13.4 us
  Pallas kernels  12.2 us (90%)
  between operations  0.66 us (5%)
  local copies, waits for them, and re-layouts  0.6 us (4%)
    pallas_call x1, Pallas kernels, per_device(): pl.pallas_call(functools.partial(kernel, n_row, n_col, slots, piece_len),...  12.2 us
    unnamed x1, local copies, waits for them, and re-layouts  0.6 us

profile of v2, /device:TPU:0, one launch (start us, length us, event | category | flops | bytes accessed | tf_op | source)
XLA Modules:
  0.0 13.4 jit_solution(14540798758497283823)
XLA Ops:
  0.7 12.2 %lanczos.1 = f32[16,128]{1,0:T(8,128)S(1)} custom-call(bf16[16,128]{1,0:T(8,128)(2,1)} %bitcast.13, bf16[32,4096]{1,0:T(8,128)(2,1)} %bitcast.12, s32[1,1,32]{2,1,0:T(1,128)} %rows_hbm.1, s32[1,1,32]{2,1,0:T(1,128)} %cols_hbm.1, s32[1,1,32]{2,1,0:T(1,128)} %scale_hbm.1, s32[1,1]{1,0:T(1,128)S(6)} %copy.12.count_sm, f32[64]{0:T(128)} %table_hbm.1), custom_call_target="tpu_custom_call" | custom-call | tf_op jit(solution)/shard_map/lanczos/pallas_call | solution.py:248
  12.8 0.6 %copy.11 = f32[4,512]{1,0:T(4,128)} copy(f32[4,512]{1,0:T(4,128)S(1)} %bitcast.11) | data formatting | bytes 16384

commit v3 on v2

v3 whole, which is shorter than its diff:
```python
import functools

import jax
import jax.numpy as jnp
from jax import lax
from jax.experimental import pallas as pl
from jax.experimental.pallas import tpu as pltpu
from jax.sharding import PartitionSpec as P

TILE = 64
NVEC = 4
LANES = 128
MESH = pl.DeviceIdType.MESH


def relayout(slots, tv_vm, w_vm):
    across = slots // 2
    pack = LANES // TILE
    step = max(1, 2 * LANES // (pack * across))
    depth = pack * step * across
    r = lax.broadcasted_iota(jnp.int32, (depth, depth), 0)
    c = lax.broadcasted_iota(jnp.int32, (depth, depth), 1)
    slot, i = lax.div(r, pack * step), lax.rem(r, pack * step)
    source = (lax.rem(i, pack) * step + lax.div(i, pack)) * across + slot
    order = jnp.where(c == source, 1.0, 0.0).astype(jnp.bfloat16)
    low_half = lax.broadcasted_iota(jnp.int32, (across, LANES), 1) < TILE
    total = TILE * TILE // LANES
    for first in range(0, total, step):
        even, odd = [], []
        for g in range(first, first + step):
            part = tv_vm[:, g * LANES:(g + 1) * LANES].astype(jnp.float32)
            turned = pltpu.roll(part, TILE, 1)
            even.append(jnp.where(low_half, part[:across], turned[across:]).astype(jnp.bfloat16))
            odd.append(jnp.where(low_half, turned[:across], part[across:]).astype(jnp.bfloat16))
        moved = jnp.dot(
            order, jnp.concatenate(even + odd, axis=0), preferred_element_type=jnp.float32)
        w_vm[:, first * pack:(first + step) * pack, :] = moved.reshape(
            across, pack * step, LANES).astype(jnp.bfloat16)


def kernel(
    n_row, n_col, slots, piece_len,
    x_hbm, w_hbm, rows_hbm, cols_hbm, scale_hbm, count_sm, table_hbm,
    out_ref,
    near_vm, far_vm, tv_vm, w_vm, index_sm, table_sm, spot_sm,
    rid_vm, cid_vm, wt_vm, pick_vm, row_send, col_send, part_vm,
    ready_sem, own_sem, index_sem, table_sem, x_send, x_row_sem, x_col_sem, p_send, p_sem,
):
    me_row = lax.axis_index("row")
    me_col = lax.axis_index("col")
    blocks = piece_len // TILE
    chunk = piece_len * NVEC // LANES
    depth = slots * NVEC
    peers = n_row + n_col - 2
    groups = piece_len // LANES

    def piece(ref, slot):
        return ref.at[pl.ds(slot * groups, groups)]

    def arrived(ref, sem):
        pltpu.make_async_copy(ref, ref, sem).wait()

    def along_col(p):
        return (me_row, p)

    def along_row(p):
        return (p, me_col)

    quarter = n_row // 4

    def between(place, n):
        return jnp.where(lax.div(place, quarter) == n, 1, 0)

    def each(low, greet, act):
        cols = [(p, me_col, n_col, along_col) for p in range(n_col)]
        rows = [(p, me_row, n_row, along_row) for p in range(n_row)]
        if not low:
            cols, rows = cols[::-1], rows[::-1]
        for p, me, total, where in cols[:1] + rows[:1] + cols[1:2] + rows[1:] + cols[2:]:
            if (low and p == total - 1) or (not low and p == 0):
                continue
            meets = p < me if low else p > me
            level = p // quarter
            if where is along_row and level in (1, 2):
                unlike = lax.div(me, quarter) != 3 - level
                apart = jnp.logical_and(meets, unlike)
                late = jnp.logical_or(meets, lax.div(me, quarter) == 3 - level)
                meets = apart if low or greet else late
            pl.when(meets)(functools.partial(act, p, where, where is along_col))

    barrier = pltpu.get_barrier_semaphore()

    def enter(p, place, is_col):
        pl.semaphore_signal(barrier, inc=1, device_id=place(p), device_id_type=MESH)

    def answer(p, place, is_col):
        pl.semaphore_signal(ready_sem, inc=1, device_id=place(p), device_id_type=MESH)

    def spread(p, place, is_col):
        pltpu.make_async_remote_copy(
            src_ref=piece(near_vm, me_col),
            dst_ref=piece(near_vm, me_col) if is_col else piece(far_vm, me_row), send_sem=x_send,
            recv_sem=x_row_sem if is_col else x_col_sem,
            device_id=place(p), device_id_type=MESH).start()

    own = pltpu.make_async_copy(x_hbm, piece(near_vm, me_col), own_sem)
    again = pltpu.make_async_copy(x_hbm, piece(far_vm, me_row), x_col_sem)
    tiles_in = pltpu.make_async_copy(w_hbm, tv_vm, own_sem)
    table_in = pltpu.make_async_copy(table_hbm, table_sm, table_sem)
    own.start()
    each(False, True, enter)
    again.start()
    for i, src in enumerate((rows_hbm, cols_hbm, scale_hbm)):
        pltpu.make_async_copy(src, index_sm.at[i], index_sem).start()
    table_in.start()
    lower = me_row + me_col - quarter * between(me_row, 2)
    higher = peers - me_row - me_col - quarter * between(me_row, 1)

    @pl.when(lower > 0)
    def _():
        pl.semaphore_wait(barrier, lower)

    each(True, True, answer)
    own.wait()
    tiles_in.start()
    each(True, False, spread)

    @pl.when(higher > 0)
    def _():
        pl.semaphore_wait(ready_sem, higher)

    each(False, False, spread)

    tiles_in.wait()
    relayout(slots, tv_vm, w_vm)
    arrived(index_sm, index_sem)
    table_in.wait()
    for t in range(slots):
        spot_sm[0, t] = lax.shift_right_logical(index_sm[0, 0, 0, t], 1)
        spot_sm[1, t] = lax.shift_right_logical(index_sm[1, 0, 0, t], 1)
    upper = lax.broadcasted_iota(jnp.int32, (8, LANES), 0) < NVEC
    for v in range(slots // 2):
        a, b = 2 * v, 2 * v + 1
        here = pl.ds(8 * v, 8)
        rid_vm[here, :] = jnp.where(upper, index_sm[0, 0, 0, a], index_sm[0, 0, 0, b])
        cid_vm[here, :] = jnp.where(upper, index_sm[1, 0, 0, a], index_sm[1, 0, 0, b])
        wt_vm[here, :] = jnp.where(
            upper, table_sm[index_sm[2, 0, 0, a]], table_sm[index_sm[2, 0, 0, b]])
    rid = rid_vm[...]
    cid = cid_vm[...]
    sub = lax.broadcasted_iota(jnp.int32, (depth, LANES), 0)
    lane = lax.broadcasted_iota(jnp.int32, (depth, LANES), 1)
    half = lax.div(lane, TILE)
    cid_piece, cid_block = lax.div(cid, blocks), lax.rem(cid, blocks)
    global_row = me_row * (n_col * blocks) + rid
    global_col = (cid_piece * n_col + me_col) * blocks + cid_block
    weight = jnp.where(global_row == global_col, 0.5, 1.0) * wt_vm[...]
    weight = jnp.where(lax.div(sub, NVEC) < count_sm[0, 0], weight, 0.0)

    pair = 2 * NVEC
    first = lax.div(sub, depth // 2)
    second = lax.rem(lax.div(sub, NVEC), 2)

    def turn(values):
        return jnp.concatenate([
            pltpu.roll(values[v * pair:(v + 1) * pair], NVEC, 0)
            for v in range(slots // 2)], axis=0)

    def places(block):
        spot = lax.div(block, 2)
        line, part = lax.div(spot, 2), lax.rem(spot, 2)
        stay = jnp.where(part == second, line, -1)
        move = turn(jnp.where(part != second, line, -1))
        return stay, move, lax.rem(block, 2)

    stay_row, move_row, odd_row = places(rid)
    stay_col, move_col, odd_col = places(cid)
    row_weight = jnp.where(half == odd_row, weight, 0.0)
    col_weight = jnp.where(half == odd_col, weight, 0.0)

    def pick(x_vm, which, odd, want):
        for t in range(slots):
            pick_vm[t * NVEC:(t + 1) * NVEC, :] = x_vm[spot_sm[which, t]].astype(jnp.float32)
        both = pick_vm[...]
        moved = jnp.where(odd == want, both, pltpu.roll(both, TILE, 1))
        return jnp.where(half == want, moved, 0.0)

    def finish(values, odd, have, weights):
        return jnp.where(odd == have, values, pltpu.roll(values, TILE, 1)) * weights

    def place(k, stay, move, values, turned):
        lines = []
        for n in range(chunk // pair):
            line = k * (chunk // pair) + n
            terms = [
                jnp.where(at[v * pair:(v + 1) * pair] == line, of[v * pair:(v + 1) * pair], 0.0)
                for v in range(slots // 2) for at, of in ((stay, values), (move, turned))]
            while len(terms) > 1:
                terms = [sum(terms[i + 1:i + 2], terms[i]) for i in range(0, len(terms), 2)]
            lines.append(terms[0])
        return jnp.concatenate(lines, axis=0)

    sets = slots // 16
    blank = jnp.zeros((2 * pair, LANES), jnp.bfloat16)

    def at(b0, m, b1, a1):
        return ((b0 * sets + m) * 2 + b1) * 2 + a1

    def left(rows, spots):
        def two(group):
            return jnp.concatenate(
                [rows[v * pair:(v + 1) * pair] for v in group], axis=0).astype(jnp.bfloat16)
        return jnp.concatenate([
            jnp.concatenate([two(spots[0]), blank], axis=1),
            jnp.concatenate([blank, two(spots[1])], axis=1)], axis=0)

    def tiles(m):
        return jnp.concatenate([
            w_vm[(m * 2 + b1) * 4:(m * 2 + b1) * 4 + 4].reshape(4 * TILE, LANES)
            for b1 in range(2)], axis=1)

    def collect(found, spots, result):
        for n, v in enumerate(spots[0] + spots[1]):
            found[v] = result[n * pair:(n + 1) * pair]

    def scatter(me, total, where, source, first, sem, stay, move, values):
        turned = turn(values)
        for k in range(total):
            source[k] = place(k, stay, move, values, turned)

            @pl.when(me != k)
            def _():
                slot = first + lax.rem(me - k + total, total) - 1
                pltpu.make_async_remote_copy(
                    src_ref=source.at[k], dst_ref=part_vm.at[slot], send_sem=p_send,
                    recv_sem=sem, device_id=where(k), device_id_type=MESH).start()

    def forward():
        arrived(far_vm, x_col_sem)
        distant = pick(far_vm, 1, odd_col, first)
        found = [None] * (slots // 2)
        for m in range(sets):
            spots = [[[at(b0, m, b1, a1) for b0 in range(2)] for b1 in range(2)]
                     for a1 in range(2)]
            result = lax.dot_general(
                jnp.concatenate([left(distant, spots[0]), left(distant, spots[1])], axis=0),
                tiles(m), (((1,), (1,)), ((), ())), preferred_element_type=jnp.float32)
            for a1 in range(2):
                collect(found, spots[a1], result[
                    a1 * 4 * pair:(a1 + 1) * 4 * pair, a1 * LANES:(a1 + 1) * LANES])
        values = finish(jnp.concatenate(found, axis=0), odd_row, second, row_weight)
        scatter(me_col, n_col, along_col, row_send, 0, p_sem, stay_row, move_row, values)

    def mirrored():
        arrived(near_vm.at[pl.ds(0, (n_col - 1) * groups)], x_row_sem)
        near = pick(near_vm, 0, odd_row, second)
        found = [None] * (slots // 2)
        for m in range(sets):
            spots = [[[at(b0, m, b1, a1) for b0 in range(2)] for a1 in range(2)]
                     for b1 in range(2)]
            result = jnp.dot(
                jnp.concatenate([left(near, spots[0]), left(near, spots[1])], axis=0),
                tiles(m), preferred_element_type=jnp.float32)
            for b1 in range(2):
                collect(found, spots[b1], result[
                    b1 * 4 * pair:(b1 + 1) * 4 * pair, b1 * LANES:(b1 + 1) * LANES])
        values = finish(jnp.concatenate(found, axis=0), odd_col, first, col_weight)
        scatter(
            me_row, n_row, along_row, col_send, n_col - 1, p_sem, stay_col, move_col, values)

    @pl.when(me_col == 0)
    def _():
        mirrored()
        forward()

    @pl.when(me_col > 0)
    def _():
        forward()
        mirrored()

    total = row_send[me_col] + col_send[me_row]
    arrived(part_vm.at[pl.ds(0, peers // 2)], x_send)
    arrived(part_vm, p_sem)
    for d in range(peers):
        total = total + part_vm[d]
    out_ref[...] = total
    arrived(part_vm, p_send)


def per_device(vectors, tile_values, tile_rows, tile_cols, tile_scale, tile_count, scale_table):
    n_row = lax.axis_size("row")
    n_col = lax.axis_size("col")
    piece_len = vectors.shape[1]
    slots = tile_rows.shape[-1]
    groups = piece_len // LANES
    chunk = groups * NVEC
    depth = slots * NVEC
    x = vectors.reshape(NVEC, groups, LANES).transpose(1, 0, 2)
    w = tile_values.reshape(slots, TILE * TILE)
    dma = pltpu.SemaphoreType.DMA
    hbm = pl.BlockSpec(memory_space=pltpu.HBM)
    out = pl.pallas_call(
        functools.partial(kernel, n_row, n_col, slots, piece_len),
        out_shape=pltpu.VMEM((chunk, LANES), jnp.float32),
        in_specs=[hbm] * 5 + [pl.BlockSpec(memory_space=pltpu.SMEM), hbm],
        out_specs=pl.BlockSpec(memory_space=pltpu.VMEM),
        scratch_shapes=[
            pltpu.VMEM((n_col * groups, NVEC, LANES), jnp.bfloat16),
            pltpu.VMEM((n_row * groups, NVEC, LANES), jnp.bfloat16),
            pltpu.VMEM((slots, TILE * TILE), jnp.bfloat16),
            pltpu.VMEM((slots // 2, TILE, LANES), jnp.bfloat16),
            pltpu.SMEM((3,) + tile_rows.shape, jnp.int32),
            pltpu.SMEM(scale_table.shape, jnp.float32),
            pltpu.SMEM((2, slots), jnp.int32),
            pltpu.VMEM((depth, LANES), jnp.int32),
            pltpu.VMEM((depth, LANES), jnp.int32),
            pltpu.VMEM((depth, LANES), jnp.float32),
            pltpu.VMEM((depth, LANES), jnp.float32),
            pltpu.VMEM((n_col, chunk, LANES), jnp.float32),
            pltpu.VMEM((n_row, chunk, LANES), jnp.float32),
            pltpu.VMEM((n_col + n_row - 2, chunk, LANES), jnp.float32),
            pltpu.SemaphoreType.REGULAR, dma, dma, dma, dma, dma, dma, dma, dma,
        ],
        compiler_params=pltpu.CompilerParams(collective_id=0, has_side_effects=True),
        name="lanczos",
    )(x, w, tile_rows, tile_cols, tile_scale, tile_count, scale_table)
    return out.reshape(groups, NVEC, LANES).transpose(1, 0, 2).reshape(NVEC, piece_len)


def solution(mesh):
    return jax.shard_map(
        per_device,
        mesh=mesh,
        in_specs=(
            P(None, ("row", "col")),
            P("row", "col", None, None),
            P("row", "col", None),
            P("row", "col", None),
            P("row", "col", None),
            P("row", "col"),
            P(),
        ),
        out_specs=P(None, ("row", "col")),
        check_vma=False,
    )
```

time: 13.6 us -> 13.3 us (0.978)
  Pallas kernels: 12.2 us -> 11.9 us
    pallas_call x1, Pallas kernels: 12.2 us -> 11.9 us  [per_device(): pl.pallas_call(functools.partial(kernel, n_row, n_col, slots, piece_len),...]
where the time goes in v3:
time: 13.3 us; the launch traced here: 13.1 us
  Pallas kernels  11.9 us (89%)
  between operations  0.66 us (5%)
  local copies, waits for them, and re-layouts  0.6 us (5%)
    pallas_call x1, Pallas kernels, per_device(): pl.pallas_call(functools.partial(kernel, n_row, n_col, slots, piece_len),...  11.9 us
    unnamed x1, local copies, waits for them, and re-layouts  0.6 us

profile of v3, /device:TPU:0, one launch (start us, length us, event | category | flops | bytes accessed | tf_op | source)
XLA Modules:
  0.0 13.1 jit_solution(9219525859913757792)
XLA Ops:
  0.7 11.9 %lanczos.1 = f32[16,128]{1,0:T(8,128)S(1)} custom-call(bf16[4,4,128]{2,1,0:T(4,128)(2,1)} %bitcast.11, bf16[32,4096]{1,0:T(8,128)(2,1)} %bitcast.10, s32[1,1,32]{2,1,0:T(1,128)} %rows_hbm.1, s32[1,1,32]{2,1,0:T(1,128)} %cols_hbm.1, s32[1,1,32]{2,1,0:T(1,128)} %scale_hbm.1, s32[1,1]{1,0:T(1,128)S(6)} %copy.11.count_sm, f32[64]{0:T(128)} %table_hbm.1), custom_call_target="tpu_custom_call" | custom-call | tf_op jit(solution)/shard_map/lanczos/pallas_call | solution.py:302
  12.5 0.6 %copy.10 = f32[4,512]{1,0:T(4,128)} copy(f32[4,512]{1,0:T(4,128)S(1)} %bitcast.9) | data formatting | bytes 16384

commit v4 on v3

--- a/solution.py
+++ b/solution.py
@@ -44,7 +44,7 @@
     out_ref,
     near_vm, far_vm, tv_vm, w_vm, index_sm, table_sm, spot_sm,
     rid_vm, cid_vm, wt_vm, pick_vm, row_send, col_send, part_vm,
-    ready_sem, own_sem, index_sem, table_sem, x_send, x_row_sem, x_col_sem, p_send, p_sem,
+    ready_sem, own_sem, index_sem, send_sem, x_row_sem, x_col_sem, p_sem,
 ):
     me_row = lax.axis_index("row")
     me_col = lax.axis_index("col")
@@ -99,20 +99,19 @@
     def spread(p, place, is_col):
         pltpu.make_async_remote_copy(
             src_ref=piece(near_vm, me_col),
-            dst_ref=piece(near_vm, me_col) if is_col else piece(far_vm, me_row), send_sem=x_send,
+            dst_ref=piece(near_vm, me_col) if is_col else piece(far_vm, me_row), send_sem=send_sem,
             recv_sem=x_row_sem if is_col else x_col_sem,
             device_id=place(p), device_id_type=MESH).start()
 
     own = pltpu.make_async_copy(x_hbm, piece(near_vm, me_col), own_sem)
     again = pltpu.make_async_copy(x_hbm, piece(far_vm, me_row), x_col_sem)
     tiles_in = pltpu.make_async_copy(w_hbm, tv_vm, own_sem)
-    table_in = pltpu.make_async_copy(table_hbm, table_sm, table_sem)
+    table_in = pltpu.make_async_copy(table_hbm, table_sm, index_sem)
     own.start()
     each(False, True, enter)
     again.start()
     for i, src in enumerate((rows_hbm, cols_hbm, scale_hbm)):
         pltpu.make_async_copy(src, index_sm.at[i], index_sem).start()
-    table_in.start()
     lower = me_row + me_col - quarter * between(me_row, 2)
     higher = peers - me_row - me_col - quarter * between(me_row, 1)
 
@@ -122,8 +121,10 @@
 
     each(True, True, answer)
     own.wait()
+    each(True, False, spread)
     tiles_in.start()
-    each(True, False, spread)
+    arrived(index_sm, index_sem)
+    table_in.start()
 
     @pl.when(higher > 0)
     def _():
@@ -133,7 +134,6 @@
 
     tiles_in.wait()
     relayout(slots, tv_vm, w_vm)
-    arrived(index_sm, index_sem)
     table_in.wait()
     for t in range(slots):
         spot_sm[0, t] = lax.shift_right_logical(index_sm[0, 0, 0, t], 1)
@@ -161,16 +161,11 @@
     first = lax.div(sub, depth // 2)
     second = lax.rem(lax.div(sub, NVEC), 2)
 
-    def turn(values):
-        return jnp.concatenate([
-            pltpu.roll(values[v * pair:(v + 1) * pair], NVEC, 0)
-            for v in range(slots // 2)], axis=0)
-
     def places(block):
         spot = lax.div(block, 2)
         line, part = lax.div(spot, 2), lax.rem(spot, 2)
         stay = jnp.where(part == second, line, -1)
-        move = turn(jnp.where(part != second, line, -1))
+        move = jnp.where(part != second, line, -1)
         return stay, move, lax.rem(block, 2)
 
     stay_row, move_row, odd_row = places(rid)
@@ -188,17 +183,19 @@
     def finish(values, odd, have, weights):
         return jnp.where(odd == have, values, pltpu.roll(values, TILE, 1)) * weights
 
-    def place(k, stay, move, values, turned):
-        lines = []
-        for n in range(chunk // pair):
-            line = k * (chunk // pair) + n
+    def place(k, stay, move, values):
+        def total(at, line):
             terms = [
-                jnp.where(at[v * pair:(v + 1) * pair] == line, of[v * pair:(v + 1) * pair], 0.0)
-                for v in range(slots // 2) for at, of in ((stay, values), (move, turned))]
+                jnp.where(at[v * pair:(v + 1) * pair] == line, values[v * pair:(v + 1) * pair], 0.0)
+                for v in range(slots // 2)]
             while len(terms) > 1:
                 terms = [sum(terms[i + 1:i + 2], terms[i]) for i in range(0, len(terms), 2)]
-            lines.append(terms[0])
-        return jnp.concatenate(lines, axis=0)
+            return terms[0]
+
+        each = chunk // pair
+        return jnp.concatenate([
+            total(stay, line) + pltpu.roll(total(move, line), NVEC, 0)
+            for line in range(k * each, (k + 1) * each)], axis=0)
 
     sets = slots // 16
     blank = jnp.zeros((2 * pair, LANES), jnp.bfloat16)
@@ -223,19 +220,22 @@
         for n, v in enumerate(spots[0] + spots[1]):
             found[v] = result[n * pair:(n + 1) * pair]
 
-    def scatter(me, total, where, source, first, sem, stay, move, values):
-        turned = turn(values)
+    def scatter(me, total, where, source, first, stay, move, values, other):
         for k in range(total):
-            source[k] = place(k, stay, move, values, turned)
-
-            @pl.when(me != k)
-            def _():
+            source[k] = place(k, stay, move, values)
+
+            def send(k=k):
                 slot = first + lax.rem(me - k + total, total) - 1
                 pltpu.make_async_remote_copy(
-                    src_ref=source.at[k], dst_ref=part_vm.at[slot], send_sem=p_send,
-                    recv_sem=sem, device_id=where(k), device_id_type=MESH).start()
-
-    def forward():
+                    src_ref=source.at[k], dst_ref=part_vm.at[slot], send_sem=send_sem,
+                    recv_sem=p_sem, device_id=where(k), device_id_type=MESH).start()
+
+            if k == 0 and other:
+                send()
+            else:
+                pl.when(me != k)(send)
+
+    def forward(other):
         arrived(far_vm, x_col_sem)
         distant = pick(far_vm, 1, odd_col, first)
         found = [None] * (slots // 2)
@@ -249,7 +249,7 @@
                 collect(found, spots[a1], result[
                     a1 * 4 * pair:(a1 + 1) * 4 * pair, a1 * LANES:(a1 + 1) * LANES])
         values = finish(jnp.concatenate(found, axis=0), odd_row, second, row_weight)
-        scatter(me_col, n_col, along_col, row_send, 0, p_sem, stay_row, move_row, values)
+        scatter(me_col, n_col, along_col, row_send, 0, stay_row, move_row, values, other)
 
     def mirrored():
         arrived(near_vm.at[pl.ds(0, (n_col - 1) * groups)], x_row_sem)
@@ -266,25 +266,26 @@
                     b1 * 4 * pair:(b1 + 1) * 4 * pair, b1 * LANES:(b1 + 1) * LANES])
         values = finish(jnp.concatenate(found, axis=0), odd_col, first, col_weight)
         scatter(
-            me_row, n_row, along_row, col_send, n_col - 1, p_sem, stay_col, move_col, values)
+            me_row, n_row, along_row, col_send, n_col - 1, stay_col, move_col, values, False)
+
+    arrived(part_vm.at[pl.ds(0, peers // 2)], send_sem)
 
     @pl.when(me_col == 0)
     def _():
         mirrored()
-        forward()
+        forward(False)
 
     @pl.when(me_col > 0)
     def _():
-        forward()
+        forward(True)
         mirrored()
 
     total = row_send[me_col] + col_send[me_row]
-    arrived(part_vm.at[pl.ds(0, peers // 2)], x_send)
     arrived(part_vm, p_sem)
     for d in range(peers):
         total = total + part_vm[d]
     out_ref[...] = total
-    arrived(part_vm, p_send)
+    arrived(part_vm, send_sem)
 
 
 def per_device(vectors, tile_values, tile_rows, tile_cols, tile_scale, tile_count, scale_table):
@@ -319,7 +320,7 @@
             pltpu.VMEM((n_col, chunk, LANES), jnp.float32),
             pltpu.VMEM((n_row, chunk, LANES), jnp.float32),
             pltpu.VMEM((n_col + n_row - 2, chunk, LANES), jnp.float32),
-            pltpu.SemaphoreType.REGULAR, dma, dma, dma, dma, dma, dma, dma, dma,
+            pltpu.SemaphoreType.REGULAR, dma, dma, dma, dma, dma, dma,
         ],
         compiler_params=pltpu.CompilerParams(collective_id=0, has_side_effects=True),
         name="lanczos",

time: 13.3 us -> 13.3 us (level)
  no operation moved by 1% of the time
where the time goes in v4:
time: 13.3 us; the launch traced here: 13.1 us
  Pallas kernels  11.9 us (89%)
  between operations  0.66 us (5%)
  local copies, waits for them, and re-layouts  0.6 us (5%)
    pallas_call x1, Pallas kernels, per_device(): pl.pallas_call(functools.partial(kernel, n_row, n_col, slots, piece_len),...  11.9 us
    unnamed x1, local copies, waits for them, and re-layouts  0.6 us

profile of v4, /device:TPU:0, one launch (start us, length us, event | category | flops | bytes accessed | tf_op | source)
XLA Modules:
  0.0 13.1 jit_solution(13100979550412677703)
XLA Ops:
  0.7 11.9 %lanczos.1 = f32[16,128]{1,0:T(8,128)S(1)} custom-call(bf16[4,4,128]{2,1,0:T(4,128)(2,1)} %bitcast.11, bf16[32,4096]{1,0:T(8,128)(2,1)} %bitcast.10, s32[1,1,32]{2,1,0:T(1,128)} %rows_hbm.1, s32[1,1,32]{2,1,0:T(1,128)} %cols_hbm.1, s32[1,1,32]{2,1,0:T(1,128)} %scale_hbm.1, s32[1,1]{1,0:T(1,128)S(6)} %copy.11.count_sm, f32[64]{0:T(128)} %table_hbm.1), custom_call_target="tpu_custom_call" | custom-call | tf_op jit(solution)/shard_map/lanczos/pallas_call | solution.py:303
  12.5 0.6 %copy.10 = f32[4,512]{1,0:T(4,128)} copy(f32[4,512]{1,0:T(4,128)S(1)} %bitcast.9) | data formatting | bytes 16384

commit v5 on v4

--- a/solution.py
+++ b/solution.py
@@ -43,7 +43,7 @@
     x_hbm, w_hbm, rows_hbm, cols_hbm, scale_hbm, count_sm, table_hbm,
     out_ref,
     near_vm, far_vm, tv_vm, w_vm, index_sm, table_sm, spot_sm,
-    rid_vm, cid_vm, wt_vm, pick_vm, row_send, col_send, part_vm,
+    rid_vm, cid_vm, wt_vm, pick_vm, lead_vm, row_send, col_send, part_vm,
     ready_sem, own_sem, index_sem, send_sem, x_row_sem, x_col_sem, p_sem,
 ):
     me_row = lax.axis_index("row")
@@ -180,19 +180,37 @@
         moved = jnp.where(odd == want, both, pltpu.roll(both, TILE, 1))
         return jnp.where(half == want, moved, 0.0)
 
-    def finish(values, odd, have, weights):
-        return jnp.where(odd == have, values, pltpu.roll(values, TILE, 1)) * weights
+    each = chunk // pair
+    for way, stay, move, weights in (
+            (0, stay_row, move_row, row_weight), (1, stay_col, move_col, col_weight)):
+        for line in range(each):
+            lead_vm[way, 2 * line] = jnp.where(stay == line, weights, 0.0)
+            lead_vm[way, 2 * line + 1] = jnp.where(move == line, weights, 0.0)
+
+    def finish(values, odd, have):
+        return jnp.where(odd == have, values, pltpu.roll(values, TILE, 1))
+
+    def tree(terms):
+        while len(terms) > 1:
+            terms = [sum(terms[i + 1:i + 2], terms[i]) for i in range(0, len(terms), 2)]
+        return terms[0]
+
+    def blocks_of(values):
+        return [values[v * pair:(v + 1) * pair] for v in range(slots // 2)]
+
+    def place_first(way, values):
+        def total(n):
+            return tree([a * b for a, b in zip(blocks_of(values), blocks_of(lead_vm[way, n]))])
+
+        return jnp.concatenate([
+            total(2 * line) + pltpu.roll(total(2 * line + 1), NVEC, 0)
+            for line in range(each)], axis=0)
 
     def place(k, stay, move, values):
         def total(at, line):
-            terms = [
-                jnp.where(at[v * pair:(v + 1) * pair] == line, values[v * pair:(v + 1) * pair], 0.0)
-                for v in range(slots // 2)]
-            while len(terms) > 1:
-                terms = [sum(terms[i + 1:i + 2], terms[i]) for i in range(0, len(terms), 2)]
-            return terms[0]
-
-        each = chunk // pair
+            return tree([
+                jnp.where(a == line, b, 0.0) for a, b in zip(blocks_of(at), blocks_of(values))])
+
         return jnp.concatenate([
             total(stay, line) + pltpu.roll(total(move, line), NVEC, 0)
             for line in range(k * each, (k + 1) * each)], axis=0)
@@ -220,20 +238,28 @@
         for n, v in enumerate(spots[0] + spots[1]):
             found[v] = result[n * pair:(n + 1) * pair]
 
-    def scatter(me, total, where, source, first, stay, move, values, other):
-        for k in range(total):
-            source[k] = place(k, stay, move, values)
-
-            def send(k=k):
+    def scatter(me, total, where, source, first, way, stay, move, weights, values, other):
+        def part(k, placed, sure=False):
+            source[k] = placed
+
+            def send():
                 slot = first + lax.rem(me - k + total, total) - 1
                 pltpu.make_async_remote_copy(
                     src_ref=source.at[k], dst_ref=part_vm.at[slot], send_sem=send_sem,
                     recv_sem=p_sem, device_id=where(k), device_id_type=MESH).start()
 
-            if k == 0 and other:
+            if sure:
                 send()
             else:
                 pl.when(me != k)(send)
+
+        part(0, place_first(way, values), other)
+
+        @pl.when(me >= 0)
+        def _():
+            weighted = values * weights
+            for k in range(1, total):
+                part(k, place(k, stay, move, weighted))
 
     def forward(other):
         arrived(far_vm, x_col_sem)
@@ -248,8 +274,9 @@
             for a1 in range(2):
                 collect(found, spots[a1], result[
                     a1 * 4 * pair:(a1 + 1) * 4 * pair, a1 * LANES:(a1 + 1) * LANES])
-        values = finish(jnp.concatenate(found, axis=0), odd_row, second, row_weight)
-        scatter(me_col, n_col, along_col, row_send, 0, stay_row, move_row, values, other)
+        values = finish(jnp.concatenate(found, axis=0), odd_row, second)
+        scatter(me_col, n_col, along_col, row_send, 0, 0, stay_row, move_row, row_weight, values,
+            other)
 
     def mirrored():
         arrived(near_vm.at[pl.ds(0, (n_col - 1) * groups)], x_row_sem)
@@ -264,9 +291,10 @@
             for b1 in range(2):
                 collect(found, spots[b1], result[
                     b1 * 4 * pair:(b1 + 1) * 4 * pair, b1 * LANES:(b1 + 1) * LANES])
-        values = finish(jnp.concatenate(found, axis=0), odd_col, first, col_weight)
+        values = finish(jnp.concatenate(found, axis=0), odd_col, first)
         scatter(
-            me_row, n_row, along_row, col_send, n_col - 1, stay_col, move_col, values, False)
+            me_row, n_row, along_row, col_send, n_col - 1, 1, stay_col, move_col, col_weight, values,
+            False)
 
     arrived(part_vm.at[pl.ds(0, peers // 2)], send_sem)
 
@@ -317,6 +345,7 @@
             pltpu.VMEM((depth, LANES), jnp.int32),
             pltpu.VMEM((depth, LANES), jnp.float32),
             pltpu.VMEM((depth, LANES), jnp.float32),
+            pltpu.VMEM((2, 2 * chunk // (2 * NVEC), depth, LANES), jnp.float32),
             pltpu.VMEM((n_col, chunk, LANES), jnp.float32),
             pltpu.VMEM((n_row, chunk, LANES), jnp.float32),
             pltpu.VMEM((n_col + n_row - 2, chunk, LANES), jnp.float32),

time: 13.3 us -> 13.3 us (level)
  no operation moved by 1% of the time
where the time goes in v5:
time: 13.3 us; the launch traced here: 13.1 us
  Pallas kernels  11.8 us (89%)
  between operations  0.66 us (5%)
  local copies, waits for them, and re-layouts  0.6 us (5%)
    pallas_call x1, Pallas kernels, per_device(): pl.pallas_call(functools.partial(kernel, n_row, n_col, slots, piece_len),...  11.8 us
    unnamed x1, local copies, waits for them, and re-layouts  0.6 us

profile of v5, /device:TPU:0, one launch (start us, length us, event | category | flops | bytes accessed | tf_op | source)
XLA Modules:
  0.0 13.1 jit_solution(15555391307451386030)
XLA Ops:
  0.7 11.8 %lanczos.1 = f32[16,128]{1,0:T(8,128)S(1)} custom-call(bf16[4,4,128]{2,1,0:T(4,128)(2,1)} %bitcast.11, bf16[32,4096]{1,0:T(8,128)(2,1)} %bitcast.10, s32[1,1,32]{2,1,0:T(1,128)} %rows_hbm.1, s32[1,1,32]{2,1,0:T(1,128)} %cols_hbm.1, s32[1,1,32]{2,1,0:T(1,128)} %scale_hbm.1, s32[1,1]{1,0:T(1,128)S(6)} %copy.11.count_sm, f32[64]{0:T(128)} %table_hbm.1), custom_call_target="tpu_custom_call" | custom-call | tf_op jit(solution)/shard_map/lanczos/pallas_call | solution.py:331
  12.5 0.6 %copy.10 = f32[4,512]{1,0:T(4,128)} copy(f32[4,512]{1,0:T(4,128)S(1)} %bitcast.9) | data formatting | bytes 16384

commit v6 on v5

--- a/solution.py
+++ b/solution.py
@@ -119,9 +119,9 @@
     def _():
         pl.semaphore_wait(barrier, lower)
 
-    each(True, True, answer)
     own.wait()
     each(True, False, spread)
+    each(True, True, answer)
     tiles_in.start()
     arrived(index_sm, index_sem)
     table_in.start()

time: 13.3 us -> 13.3 us (level)
  no operation moved by 1% of the time
where the time goes in v6:
time: 13.3 us; the launch traced here: 13.1 us
  Pallas kernels  11.8 us (89%)
  between operations  0.66 us (5%)
  local copies, waits for them, and re-layouts  0.6 us (5%)
    pallas_call x1, Pallas kernels, per_device(): pl.pallas_call(functools.partial(kernel, n_row, n_col, slots, piece_len),...  11.8 us
    unnamed x1, local copies, waits for them, and re-layouts  0.6 us

profile of v6, /device:TPU:0, one launch (start us, length us, event | category | flops | bytes accessed | tf_op | source)
XLA Modules:
  0.0 13.1 jit_solution(11381834263238739255)
XLA Ops:
  0.7 11.8 %lanczos.1 = f32[16,128]{1,0:T(8,128)S(1)} custom-call(bf16[4,4,128]{2,1,0:T(4,128)(2,1)} %bitcast.11, bf16[32,4096]{1,0:T(8,128)(2,1)} %bitcast.10, s32[1,1,32]{2,1,0:T(1,128)} %rows_hbm.1, s32[1,1,32]{2,1,0:T(1,128)} %cols_hbm.1, s32[1,1,32]{2,1,0:T(1,128)} %scale_hbm.1, s32[1,1]{1,0:T(1,128)S(6)} %copy.11.count_sm, f32[64]{0:T(128)} %table_hbm.1), custom_call_target="tpu_custom_call" | custom-call | tf_op jit(solution)/shard_map/lanczos/pallas_call | solution.py:331
  12.5 0.6 %copy.10 = f32[4,512]{1,0:T(4,128)} copy(f32[4,512]{1,0:T(4,128)S(1)} %bitcast.9) | data formatting | bytes 16384

commit v7 on v6

--- a/solution.py
+++ b/solution.py
@@ -310,9 +310,7 @@
 
     total = row_send[me_col] + col_send[me_row]
     arrived(part_vm, p_sem)
-    for d in range(peers):
-        total = total + part_vm[d]
-    out_ref[...] = total
+    out_ref[...] = tree([total] + [part_vm[d] for d in range(peers)])
     arrived(part_vm, send_sem)
 
 

time: 13.3 us -> 13.3 us (level)
  no operation moved by 1% of the time
where the time goes in v7:
time: 13.3 us; the launch traced here: 13.1 us
  Pallas kernels  11.8 us (89%)
  between operations  0.66 us (5%)
  local copies, waits for them, and re-layouts  0.6 us (5%)
    pallas_call x1, Pallas kernels, per_device(): pl.pallas_call(functools.partial(kernel, n_row, n_col, slots, piece_len),...  11.8 us
    unnamed x1, local copies, waits for them, and re-layouts  0.6 us

profile of v7, /device:TPU:0, one launch (start us, length us, event | category | flops | bytes accessed | tf_op | source)
XLA Modules:
  0.0 13.1 jit_solution(15994425527118287639)
XLA Ops:
  0.7 11.8 %lanczos.1 = f32[16,128]{1,0:T(8,128)S(1)} custom-call(bf16[4,4,128]{2,1,0:T(4,128)(2,1)} %bitcast.11, bf16[32,4096]{1,0:T(8,128)(2,1)} %bitcast.10, s32[1,1,32]{2,1,0:T(1,128)} %rows_hbm.1, s32[1,1,32]{2,1,0:T(1,128)} %cols_hbm.1, s32[1,1,32]{2,1,0:T(1,128)} %scale_hbm.1, s32[1,1]{1,0:T(1,128)S(6)} %copy.11.count_sm, f32[64]{0:T(128)} %table_hbm.1), custom_call_target="tpu_custom_call" | custom-call | tf_op jit(solution)/shard_map/lanczos/pallas_call | solution.py:329
  12.5 0.6 %copy.10 = f32[4,512]{1,0:T(4,128)} copy(f32[4,512]{1,0:T(4,128)S(1)} %bitcast.9) | data formatting | bytes 16384
